TPU v7x, 32 devices: a whole 2x2x4 slice. The times are simulated.
32 devices in a mesh: dp: 4 (over x, core), fsdp: 8 (over z, y).
Axes of the slice: x: 2, y: 2, z: 4, core: 2. Of those that a mesh axis runs over, the one named last changes fastest.
Arguments:
- tokens: bfloat16 [8192, 768], P(('dp', 'fsdp')), may hold values from -6 to 6
- cotangent: bfloat16 [8192, 768], P(('dp', 'fsdp')), may hold values from -6 to 6
- starts: int32 [8192], P(('dp', 'fsdp')), may hold values from 0 to 256, as said below
- attention_norm_scale: bfloat16 [768], P(('dp', 'fsdp')), may hold values from 0.5 to 1.5
- w_qkv: bfloat16 [768, 2304], P(('dp', 'fsdp')), may hold values from -3 to 3
- w_out: bfloat16 [768, 768], P(None, ('dp', 'fsdp')), may hold values from -0.875 to 0.875
- feedforward_norm_scale: bfloat16 [768], P(('dp', 'fsdp')), may hold values from 0.5 to 1.5
- w_in: bfloat16 [768, 2304], P(('dp', 'fsdp')), may hold values from -0.21875 to 0.21875
- w_down: bfloat16 [1152, 768], P(None, ('dp', 'fsdp')), may hold values from -0.1875 to 0.1875
Outputs:
- output: bfloat16 [8192, 768], P(('dp', 'fsdp'))
- input_grad: float32 [8192, 768], P(('dp', 'fsdp'))
- w_qkv_grad: float32 [768, 2304], P(('dp', 'fsdp'))
- w_out_grad: float32 [768, 768], P(None, ('dp', 'fsdp'))
- w_in_grad: float32 [768, 2304], P(('dp', 'fsdp'))
- w_down_grad: float32 [1152, 768], P(None, ('dp', 'fsdp'))
- attn_gain_grad: float32 [768], P(('dp', 'fsdp'))
- mlp_gain_grad: float32 [768], P(('dp', 'fsdp'))
Inputs may be any that keep to these rules, and one draw needn't show every extreme that they name: `starts`: each sequence lies whole in one block of 256 slots and occupies consecutive slots; a slot's entry is its sequence's first slot within the block. Slots after a block's last sequence are empty and hold 256. In every draw some block has no empty slot and some other block has one or more.
All inputs are finite; a program needn't handle non-finite values.
Results may differ from a plain program's by a relative error of at most 0.012.
Values may be sent and summed in bfloat16 or wider, within the bound.
A program may use at most 128 MiB of HBM per device.

v0:
```python
import jax
import jax.numpy as jnp
from jax import lax
from jax.sharding import PartitionSpec as P

HEAD_DIM = 64
HALF_WINDOW = 64


epsilon = 1e-05
rope_base = 10000.0
sqrt_half = 0.7071067811865476
inv_sqrt_tau = 0.3989422804014327
big_negative = -1e30


def apply_layer_norm(values):
    mean_value = jnp.mean(values, axis=-1, keepdims=True)
    centered = values - mean_value
    inverse_deviation = lax.rsqrt(jnp.mean(centered * centered, axis=-1, keepdims=True) + epsilon)
    return (centered * inverse_deviation, inverse_deviation)


def norm_backward(normalized_gradient, standardized_input, inverse_deviation, norm_scale):
    scale_gradient = jnp.sum(normalized_gradient * standardized_input, axis=0)
    scaled_output = normalized_gradient * norm_scale
    first_average = jnp.mean(scaled_output, axis=-1, keepdims=True)
    second_average = jnp.mean(scaled_output * standardized_input, axis=-1, keepdims=True)
    return (
        inverse_deviation * (scaled_output - first_average - standardized_input * second_average),
        scale_gradient,
    )


def gelu_parts(pre_act):
    normal_cdf = 0.5 * (1.0 + jax.scipy.special.erf(pre_act * sqrt_half))
    density = jnp.exp(-0.5 * pre_act * pre_act) * inv_sqrt_tau
    return (pre_act * normal_cdf, normal_cdf + pre_act * density)


def rotary_tables(position, head_dim):
    half_dim = head_dim // 2
    exponent = 2.0 * jnp.arange(half_dim).astype(jnp.float32) / head_dim
    frequency = rope_base ** (-exponent)
    angle = position.astype(jnp.float32)[:, None] * frequency[None, :]
    return (jnp.cos(angle), jnp.sin(angle))


def rotate(values, cosine, sine):
    half_dim = values.shape[-1] // 2
    first_half = values[..., :half_dim]
    second_half = values[..., half_dim:]
    return jnp.concatenate(
        [first_half * cosine - second_half * sine, second_half * cosine + first_half * sine], -1
    )


def unrotate(grads, cosine, sine):
    half_dim = grads.shape[-1] // 2
    first_half = grads[..., :half_dim]
    second_half = grads[..., half_dim:]
    return jnp.concatenate(
        [first_half * cosine + second_half * sine, second_half * cosine - first_half * sine], -1
    )


def contract_rows(left, right):
    return lax.dot_general(
        left, right, (((0,), (0,)), ((), ())), preferred_element_type=jnp.float32
    )


def times_transposed(left, right):
    return lax.dot_general(
        left, right, (((1,), (1,)), ((), ())), preferred_element_type=jnp.float32
    )


def body(
    tokens,
    cotangent,
    starts,
    attention_norm_scale,
    w_qkv,
    w_out,
    feedforward_norm_scale,
    w_in,
    w_down,
):
    row_count, width = tokens.shape
    head_dim = HEAD_DIM
    head_count = width // head_dim
    units = w_down.shape[0]
    scale = head_dim ** (-0.5)
    shards = (w_qkv, w_out, w_in, w_down, attention_norm_scale, feedforward_norm_scale)
    full_qkv, full_out, full_in, full_down, gathered_attention_scale, gathered_feedforward_scale = (
        lax.all_gather(shards[0], ("dp", "fsdp"), axis=0, tiled=True),
        lax.all_gather(shards[1], ("dp", "fsdp"), axis=1, tiled=True),
        lax.all_gather(shards[2], ("dp", "fsdp"), axis=0, tiled=True),
        lax.all_gather(shards[3], ("dp", "fsdp"), axis=1, tiled=True),
        lax.all_gather(shards[4], ("dp", "fsdp"), axis=0, tiled=True),
        lax.all_gather(shards[5], ("dp", "fsdp"), axis=0, tiled=True),
    )
    slot = jnp.arange(row_count, dtype=jnp.int32)
    valid = starts < row_count
    position = slot - starts
    distance = jnp.abs(slot[:, None] - slot[None, :])
    allowed = (starts[:, None] == starts[None, :]) & (distance <= HALF_WINDOW)
    input_float = tokens.astype(jnp.float32)
    first_standardized, first_inverse_deviation = apply_layer_norm(input_float)
    first_normalized = (first_standardized * gathered_attention_scale.astype(jnp.float32)).astype(
        jnp.bfloat16
    )
    projected = jnp.dot(first_normalized, full_qkv, preferred_element_type=jnp.float32)
    projected = projected.reshape(row_count, 3, head_count, head_dim).transpose(1, 2, 0, 3)
    cosine, sine = rotary_tables(position, head_dim)
    queries = rotate(projected[0], cosine, sine).astype(jnp.bfloat16)
    keys_rot = rotate(projected[1], cosine, sine).astype(jnp.bfloat16)
    values_h = projected[2].astype(jnp.bfloat16)

    def head_scores(query_h, key_h):
        scores = jnp.einsum("qd,kd->qk", query_h, key_h, preferred_element_type=jnp.float32) * scale
        return jnp.where(allowed, scores, big_negative)

    def head_forward(operands):
        query_h, key_h, value_h = operands
        scores = head_scores(query_h, key_h)
        top = jnp.max(scores, axis=-1, keepdims=True)
        log_total = top + jnp.log(jnp.sum(jnp.exp(scores - top), axis=-1, keepdims=True))
        weights_b = jnp.exp(scores - log_total).astype(jnp.bfloat16)
        attended_head = jnp.dot(weights_b, value_h, preferred_element_type=jnp.float32).astype(
            jnp.bfloat16
        )
        return (attended_head, log_total)

    attended_heads, log_totals = lax.map(head_forward, (queries, keys_rot, values_h))
    attended = attended_heads.transpose(1, 0, 2).reshape(row_count, width)
    hidden_state = input_float + jnp.dot(attended, full_out, preferred_element_type=jnp.float32)
    second_standardized, second_inverse_deviation = apply_layer_norm(hidden_state)
    second_normalized = (
        second_standardized * gathered_feedforward_scale.astype(jnp.float32)
    ).astype(jnp.bfloat16)
    gate_up = jnp.dot(second_normalized, full_in, preferred_element_type=jnp.float32)
    pre_act = gate_up[:, :units]
    gate_half = gate_up[:, units:]
    activated, slope = gelu_parts(pre_act)
    hidden = (activated * gate_half).astype(jnp.bfloat16)
    output = (hidden_state + jnp.dot(hidden, full_down, preferred_element_type=jnp.float32)).astype(
        jnp.bfloat16
    )
    back_qkv, back_out, back_in, back_down, attention_scale_backward, feedforward_scale_backward = (
        lax.all_gather(shards[0], ("dp", "fsdp"), axis=0, tiled=True),
        lax.all_gather(shards[1], ("dp", "fsdp"), axis=1, tiled=True),
        lax.all_gather(shards[2], ("dp", "fsdp"), axis=0, tiled=True),
        lax.all_gather(shards[3], ("dp", "fsdp"), axis=1, tiled=True),
        lax.all_gather(shards[4], ("dp", "fsdp"), axis=0, tiled=True),
        lax.all_gather(shards[5], ("dp", "fsdp"), axis=0, tiled=True),
    )
    grad_out = jnp.where(valid[:, None], cotangent, jnp.zeros_like(cotangent))
    down_grad_t = contract_rows(grad_out, hidden)
    d_hidden = times_transposed(grad_out, back_down)
    d_gu = jnp.concatenate([d_hidden * gate_half * slope, d_hidden * activated], 1).astype(
        jnp.bfloat16
    )
    second_normalized_gradient = times_transposed(d_gu, back_in)
    mixed_gradient, feedforward_scale_gradient = norm_backward(
        second_normalized_gradient,
        second_standardized,
        second_inverse_deviation,
        feedforward_scale_backward.astype(jnp.float32),
    )
    d_state = grad_out.astype(jnp.float32) + mixed_gradient
    d_state_b = d_state.astype(jnp.bfloat16)
    out_grad_t = contract_rows(d_state_b, attended)
    d_attended = times_transposed(d_state_b, back_out).astype(jnp.bfloat16)
    d_attended = d_attended.reshape(row_count, head_count, head_dim).transpose(1, 0, 2)

    def head_backward(operands):
        query_h, key_h, value_h, log_h, attended_head, d_att_head = operands
        scores = head_scores(query_h, key_h)
        weights_f = jnp.exp(scores - log_h)
        weights_b = weights_f.astype(jnp.bfloat16)
        delta = jnp.sum(
            d_att_head.astype(jnp.float32) * attended_head.astype(jnp.float32),
            axis=-1,
            keepdims=True,
        )
        d_weights = jnp.einsum("qd,kd->qk", d_att_head, value_h, preferred_element_type=jnp.float32)
        d_scores = (weights_f * (d_weights - delta) * scale).astype(jnp.bfloat16)
        d_value = jnp.einsum("qk,qd->kd", weights_b, d_att_head, preferred_element_type=jnp.float32)
        d_query = jnp.dot(d_scores, key_h, preferred_element_type=jnp.float32)
        d_key = jnp.einsum("qk,qd->kd", d_scores, query_h, preferred_element_type=jnp.float32)
        return (d_query, d_key, d_value)

    d_query, d_key, d_value = lax.map(
        head_backward, (queries, keys_rot, values_h, log_totals, attended_heads, d_attended)
    )
    d_joined = jnp.stack(
        [unrotate(d_query, cosine, sine), unrotate(d_key, cosine, sine), d_value], 0
    )
    d_qkv = d_joined.transpose(2, 0, 1, 3).reshape(row_count, 3 * width).astype(jnp.bfloat16)
    first_normalized_gradient = times_transposed(d_qkv, back_qkv)
    norm_input_gradient, attention_scale_gradient = norm_backward(
        first_normalized_gradient,
        first_standardized,
        first_inverse_deviation,
        attention_scale_backward.astype(jnp.float32),
    )
    input_grad = d_state + norm_input_gradient
    qkv_whole = contract_rows(first_normalized, d_qkv)
    in_whole = contract_rows(second_normalized, d_gu)
    every_grad = (
        qkv_whole,
        out_grad_t,
        in_whole,
        down_grad_t,
        attention_scale_gradient,
        feedforward_scale_gradient,
    )
    qkv_owned, out_owned_t, in_owned, down_owned_t, gain_a_owned, gain_m_owned = (
        lax.psum_scatter(every_grad[0], ("dp", "fsdp"), scatter_dimension=0, tiled=True),
        lax.psum_scatter(every_grad[1], ("dp", "fsdp"), scatter_dimension=0, tiled=True),
        lax.psum_scatter(every_grad[2], ("dp", "fsdp"), scatter_dimension=0, tiled=True),
        lax.psum_scatter(every_grad[3], ("dp", "fsdp"), scatter_dimension=0, tiled=True),
        lax.psum_scatter(every_grad[4], ("dp", "fsdp"), scatter_dimension=0, tiled=True),
        lax.psum_scatter(every_grad[5], ("dp", "fsdp"), scatter_dimension=0, tiled=True),
    )
    return (
        output,
        input_grad,
        qkv_owned,
        out_owned_t.T,
        in_owned,
        down_owned_t.T,
        gain_a_owned,
        gain_m_owned,
    )


def solution(mesh):
    return jax.shard_map(
        body,
        mesh=mesh,
        in_specs=(
            P(("dp", "fsdp"), None),
            P(("dp", "fsdp"), None),
            P(("dp", "fsdp")),
            P(("dp", "fsdp")),
            P(("dp", "fsdp"), None),
            P(None, ("dp", "fsdp")),
            P(("dp", "fsdp")),
            P(("dp", "fsdp"), None),
            P(None, ("dp", "fsdp")),
        ),
        out_specs=(
            P(("dp", "fsdp"), None),
            P(("dp", "fsdp"), None),
            P(("dp", "fsdp"), None),
            P(None, ("dp", "fsdp")),
            P(("dp", "fsdp"), None),
            P(None, ("dp", "fsdp")),
            P(("dp", "fsdp")),
            P(("dp", "fsdp")),
        ),
        check_vma=False,
    )
```

profile of v0, /device:TPU:0, one launch (start us, length us, event | category | flops | bytes accessed | tf_op | source)
XLA Modules:
  0.0 720.8 jit_solution(493266925335314583)
XLA Ops:
  13.6 42.2 %all-reduce.6 = (bf16[768]{0:T(1024)(128)(2,1)S(1)}, bf16[768]{0:T(1024)(128)(2,1)S(1)}) all-reduce(bf16[768]{0:T(1024)(128)(2,1)S(1)} %dynamic-update-slice, bf16[768]{0:T(1024)(128)(2,1)S(1)} %dynamic-update-slice.1), channel_id=1, replica_groups=mesh['dp'=4,'fsdp'=8] {'dp','fsdp'}, use_global_device_ids=true, to_apply=%add | all-reduce | flops 1536 | bytes 6144
  58.5 15.2 %all-gather.5.cloned.1.call-done = bf16[768,2304]{1,0:T(8,128)(2,1)} async-done(((bf16[24,2304]{1,0:T(8,128)(2,1)}), bf16[768,2304]{1,0:T(8,128)(2,1)}) %all-gather.5.cloned.1.call-update) | async-done | bytes 3538960 | tf_op jit(solution)/shard_map/all_gather | solution.py:97
  73.7 3.6 fusion.77
  79.8 23.4 %while.28 = (s32[]{:T(128)}, bf16[12,256,64]{1,2,0:T(8,128)(2,1)S(1)}, f32[12,256,1]{1,2,0:T(1,128)}, bf16[12,256,64]{2,1,0:T(8,128)(2,1)S(1)}, bf16[12,256,64]{...) while((s32[]{:T(128)}, ...), condition=%wide.region_5.6_spmd.clone, body=%wide.region_2.5_spmd.clone.sunk | while | flops 17579776 | bytes 1029217 | solution.py:136
  103.2 26.3 %all-gather.7.cloned.1.call-done = bf16[768,768]{0,1:T(8,128)(2,1)} async-done(((bf16[768,24]{0,1:T(8,128)(2,1)}), bf16[768,768]{0,1:T(8,128)(2,1)}) %all-gather.7.cloned.1.call-update) | async-done | bytes 1179664 | tf_op jit(solution)/shard_map/all_gather | solution.py:98
  129.5 1.9 fusion.81
  132.8 58.6 %all-gather.9.cloned.1.call-done = bf16[768,2304]{1,0:T(8,128)(2,1)} async-done(((bf16[24,2304]{1,0:T(8,128)(2,1)}), bf16[768,2304]{1,0:T(8,128)(2,1)}) %all-gather.9.cloned.1.call-update) | async-done | bytes 3538960 | tf_op jit(solution)/shard_map/all_gather | solution.py:99
  191.4 3.1 fusion.79
  194.5 54.0 %all-gather.11.cloned.1.call-done = bf16[1152,768]{0,1:T(8,128)(2,1)} async-done(((bf16[1152,24]{0,1:T(8,128)(2,1)}), bf16[1152,768]{0,1:T(8,128)(2,1)}) %all-gather.11.cloned.1.call-update) | async-done | bytes 1769488 | tf_op jit(solution)/shard_map/all_gather | solution.py:100
  248.5 3.6 fusion.51
  252.2 1.8 multiply_reduce_fusion
  255.0 2.0 fusion.68
  260.7 3.6 fusion.73
  265.0 87.8 %while.29 = (s32[]{:T(128)}, f32[12,256,64]{1,2,0:T(8,128)}, f32[12,256,64]{1,2,0:T(8,128)}, bf16[12,256,64]{1,2,0:T(8,128)(2,1)}, bf16[12,256,64]{2,1,0:T(8,128...) while((s32[]{:T(128)}, f32[12,256,64]{1,2,0:T(8,128)}, ...), condition=%wide.region_12.13_spmd.clone, body=%wide.region_10.12_spmd.clone.sunk | while | flops 42860288 | bytes 2109573 | solution.py:195
  269.9 1.7 fusion.134
  282.8 1.7 fusion.133
  355.5 4.2 fusion.75
  360.4 5.4 fusion.65
  365.8 4.2 fusion.63
  370.0 38.6 %all-reduce.5 = (f32[768]{0:T(1024)S(1)}, f32[768]{0:T(1024)S(1)}) all-reduce(f32[768]{0:T(1024)S(1)} %get-tuple-element.208, f32[768]{0:T(1024)S(1)} %copy-done.23), channel_id=6, replica_groups=mesh['dp'=4,'fsdp'=8] {'dp','fsdp'}, use_global_device_ids=true, to_apply=%region_20.21.clone | all-reduce | flops 1536 | bytes 12288
  409.7 2.5 fusion.62
  413.7 50.6 %reduce-scatter.13.cloned.1.call-done = f32[24,1152]{1,0:T(8,128)} async-done(((f32[768,1152]{1,0:T(8,128)}), f32[24,1152]{1,0:T(8,128)}) %reduce-scatter.13.cloned.1.call-update) | async-done | bytes 110608
  464.3 124.9 %reduce-scatter.7.cloned.1.call-done = f32[24,2304]{1,0:T(8,128)} async-done(((f32[768,2304]{1,0:T(8,128)}), f32[24,2304]{1,0:T(8,128)}) %reduce-scatter.7.cloned.1.call-update) | async-done | bytes 221200 | tf_op jit(solution)/shard_map/reduce_scatter | solution.py:221
  589.1 124.8 %reduce-scatter.11.cloned.1.call-done = f32[24,2304]{1,0:T(8,128)} async-done(((f32[768,2304]{1,0:T(8,128)}), f32[24,2304]{1,0:T(8,128)}) %reduce-scatter.11.cloned.1.call-update) | async-done | bytes 221200 | tf_op jit(solution)/shard_map/reduce_scatter | solution.py:223
  (292 shorter events, 131.5 us)
Async XLA Ops:
  7.2 66.5 %copy-start = (bf16[256,768]{1,0:T(8,128)(2,1)S(1)}, bf16[256,768]{1,0:T(8,128)(2,1)}, u32[]{:S(2)}) copy-start(bf16[256,768]{1,0:T(8,128)(2,1)} %param.13) | copy-start | bytes 1179652
  7.2 66.5 %all-gather.5.cloned.1.call-start = ((), (), s32[]{:S(2)}) async-start(), calls=%async_computation.4 | async-start | bytes 3649536 | tf_op jit(solution)/shard_map/all_gather | solution.py:97
  7.9 121.6 %all-gather.7.cloned.1.call-start = ((), (), s32[]{:S(2)}) async-start(), calls=%async_computation.5 | async-start | bytes 1216512 | tf_op jit(solution)/shard_map/all_gather | solution.py:98
  8.7 182.7 %all-gather.9.cloned.1.call-start = ((), (), s32[]{:S(2)}) async-start(), calls=%async_computation.6 | async-start | bytes 3649536 | tf_op jit(solution)/shard_map/all_gather | solution.py:99
  9.4 239.1 %all-gather.11.cloned.1.call-start = ((), (), s32[]{:S(2)}) async-start(), calls=%async_computation.7 | async-start | bytes 1824768 | tf_op jit(solution)/shard_map/all_gather | solution.py:100
  10.0 403.7 %reduce-scatter.9.cloned.1.call-start = ((), (), s32[]{:S(2)}) async-start(), calls=%async_computation.9 | async-start | bytes 2433024 | tf_op jit(solution)/shard_map/reduce_scatter | solution.py:222
  58.5 19.0 %copy-start.14 = (f32[256,32]{0,1:T(8,128)}, f32[256,32]{0,1:T(8,128)S(1)}, u32[]{:S(2)}) copy-start(f32[256,32]{0,1:T(8,128)S(1)} %get-tuple-element.273) | copy-start | bytes 98308
  58.5 19.0 %copy-start.16 = (f32[256,32]{0,1:T(8,128)}, f32[256,32]{0,1:T(8,128)S(1)}, u32[]{:S(2)}) copy-start(f32[256,32]{0,1:T(8,128)S(1)} %get-tuple-element.274) | copy-start | bytes 98308
  103.2 28.2 %copy-start.3 = (bf16[12,256,64]{2,1,0:T(8,128)(2,1)}, bf16[12,256,64]{2,1,0:T(8,128)(2,1)S(1)}, u32[]{:S(2)}) copy-start(bf16[12,256,64]{2,1,0:T(8,128)(2,1)S(1)} %get-tuple-element.478) | copy-start | bytes 1179652
  103.2 28.2 %copy-start.6 = (bf16[12,256,64]{1,2,0:T(8,128)(2,1)}, bf16[12,256,64]{1,2,0:T(8,128)(2,1)S(1)}, u32[]{:S(2)}) copy-start(bf16[12,256,64]{1,2,0:T(8,128)(2,1)S(1)} %get-tuple-element.432) | copy-start | bytes 1179652
  103.2 28.2 %copy-start.9 = (bf16[12,256,64]{2,1,0:T(8,128)(2,1)}, bf16[12,256,64]{2,1,0:T(8,128)(2,1)S(1)}, u32[]{:S(2)}) copy-start(bf16[12,256,64]{2,1,0:T(8,128)(2,1)S(1)} %get-tuple-element.480) | copy-start | bytes 1179652
  248.5 3.6 copy-start.2
  248.5 3.6 copy-start.19
  248.5 3.6 copy-start.21
  252.1 1.8 copy-start.11
  252.1 1.8 copy-start.12
  257.0 207.3 %reduce-scatter.13.cloned.1.call-start = ((), (), s32[]{:S(2)}) async-start(), calls=%async_computation.11 | async-start | bytes 3649536
  264.3 324.9 %reduce-scatter.7.cloned.1.call-start = ((), (), s32[]{:S(2)}) async-start(), calls=%async_computation.8 | async-start | bytes 7299072 | tf_op jit(solution)/shard_map/reduce_scatter | solution.py:221
  265.0 87.8 %copy-start.15 = (f32[256,32]{0,1:T(8,128)S(1)}, f32[256,32]{0,1:T(8,128)}, u32[]{:S(2)}) copy-start(f32[256,32]{0,1:T(8,128)} %copy-done.14) | copy-start | bytes 98308
  265.0 87.8 %copy-start.17 = (f32[256,32]{0,1:T(8,128)S(1)}, f32[256,32]{0,1:T(8,128)}, u32[]{:S(2)}) copy-start(f32[256,32]{0,1:T(8,128)} %copy-done.16) | copy-start | bytes 98308
  359.7 354.2 %reduce-scatter.11.cloned.1.call-start = ((), (), s32[]{:S(2)}) async-start(), calls=%async_computation.10 | async-start | bytes 7299072 | tf_op jit(solution)/shard_map/reduce_scatter | solution.py:223
  365.8 4.2 copy-start.23
  409.7 2.5 copy-start.5
  409.7 2.5 copy-start.8
  (11 other events, 12.3 us)
Sparse Core Ops, SparseCore 0:
  10.9 62.7 all-gather.4
  76.6 52.8 all-gather.6
  132.4 58.9 all-gather.8
  194.1 54.3 all-gather.10
  257.1 98.7 reduce-scatter.8
  361.8 102.4 reduce-scatter.12
  470.5 118.5 reduce-scatter.6
  595.4 118.4 reduce-scatter.10
where the time goes:
time: 725 us; the launch traced here: 721 us
  waiting for transfers between devices  457 us (63%)
  matrix products  126 us (17%)
  blocking collectives  80.8 us (11%)
  local copies, waits for them, and re-layouts  28.3 us (4%)
  between operations  14.5 us (2%)
  other arithmetic  12.7 us (2%)
    reduce_scatter x1, waiting for transfers between devices, body(): lax.psum_scatter(every_grad[0], ('dp', 'fsdp'), scatter_dimension=0, tile...  125 us
    reduce_scatter x1, waiting for transfers between devices, body(): lax.psum_scatter(every_grad[2], ('dp', 'fsdp'), scatter_dimension=0, tile...  125 us
    unnamed x2, blocking collectives  80.8 us
    all_gather x1, waiting for transfers between devices, body(): lax.all_gather(shards[2], ('dp', 'fsdp'), axis=0, tiled=True)  58.6 us
    all_gather x1, waiting for transfers between devices, body(): lax.all_gather(shards[3], ('dp', 'fsdp'), axis=1, tiled=True)  54 us
    unnamed x9, waiting for transfers between devices  53.2 us
    all_gather x1, waiting for transfers between devices, body(): lax.all_gather(shards[1], ('dp', 'fsdp'), axis=1, tiled=True)  26.3 us
    dot_general x24, matrix products, head_scores(): jnp.einsum('qd,kd->qk', query_h, key_h, preferred_element_type=jnp.float32)  25.9 us
  transfers between devices with their start and end apart: 8, of which 7 were waited for; matrix products, arithmetic and copies ran while one was open for 22% of the time, Pallas kernels for 0%

commit v1 on v0

v1 whole, which is shorter than its diff:
```python
import functools

import jax
import jax.numpy as jnp
from jax import lax
from jax.experimental import pallas as pl
from jax.experimental.pallas import tpu as pltpu
from jax.sharding import PartitionSpec as P

HEAD_DIM = 64
HALF_WINDOW = 64


epsilon = 1e-05
rope_base = 10000.0
sqrt_half = 0.7071067811865476
inv_sqrt_tau = 0.3989422804014327
big_negative = -1e30


def apply_layer_norm(values):
    mean_value = jnp.mean(values, axis=-1, keepdims=True)
    centered = values - mean_value
    inverse_deviation = lax.rsqrt(jnp.mean(centered * centered, axis=-1, keepdims=True) + epsilon)
    return (centered * inverse_deviation, inverse_deviation)


def norm_backward(normalized_gradient, standardized_input, inverse_deviation, norm_scale):
    scale_gradient = jnp.sum(normalized_gradient * standardized_input, axis=0)
    scaled_output = normalized_gradient * norm_scale
    first_average = jnp.mean(scaled_output, axis=-1, keepdims=True)
    second_average = jnp.mean(scaled_output * standardized_input, axis=-1, keepdims=True)
    return (
        inverse_deviation * (scaled_output - first_average - standardized_input * second_average),
        scale_gradient,
    )


def gelu_parts(pre_act):
    normal_cdf = 0.5 * (1.0 + jax.scipy.special.erf(pre_act * sqrt_half))
    density = jnp.exp(-0.5 * pre_act * pre_act) * inv_sqrt_tau
    return (pre_act * normal_cdf, normal_cdf + pre_act * density)


def rotary_tables(position, head_dim):
    half_dim = head_dim // 2
    exponent = 2.0 * jnp.arange(half_dim).astype(jnp.float32) / head_dim
    frequency = rope_base ** (-exponent)
    angle = position.astype(jnp.float32)[:, None] * frequency[None, :]
    return (jnp.cos(angle), jnp.sin(angle))


def rotate(values, cosine, sine):
    half_dim = values.shape[-1] // 2
    first_half = values[..., :half_dim]
    second_half = values[..., half_dim:]
    return jnp.concatenate(
        [first_half * cosine - second_half * sine, second_half * cosine + first_half * sine], -1
    )


def unrotate(grads, cosine, sine):
    half_dim = grads.shape[-1] // 2
    first_half = grads[..., :half_dim]
    second_half = grads[..., half_dim:]
    return jnp.concatenate(
        [first_half * cosine + second_half * sine, second_half * cosine - first_half * sine], -1
    )


def contract_rows(left, right):
    return lax.dot_general(
        left, right, (((0,), (0,)), ((), ())), preferred_element_type=jnp.float32
    )


def times_transposed(left, right):
    return lax.dot_general(
        left, right, (((1,), (1,)), ((), ())), preferred_element_type=jnp.float32
    )


MESH = pl.DeviceIdType.MESH
LANES = 128


def split_pair(count):
    inner = 2 if count % 2 == 0 else 1
    return count // inner, inner


class Grid:
    def __init__(self, dp, fsdp):
        x, c = split_pair(dp)
        z, y = split_pair(fsdp)
        self.size = {"x": x, "c": c, "z": z, "y": y}

    def here(self):
        d, f = lax.axis_index("dp"), lax.axis_index("fsdp")
        c, y = self.size["c"], self.size["y"]
        return {"x": lax.div(d, c), "c": lax.rem(d, c), "z": lax.div(f, y), "y": lax.rem(f, y)}

    def step(self, at, axis, k):
        return {**at, axis: lax.rem(at[axis] + k, self.size[axis])}

    def device(self, at):
        return (at["x"] * self.size["c"] + at["c"], at["z"] * self.size["y"] + at["y"])

    def shape(self):
        return tuple(self.size[a] for a in "xczy")

    def barrier(self, at):
        sem = pltpu.get_barrier_semaphore()
        total = 0
        for axis in "xczy":
            for k in range(1, self.size[axis]):
                pl.semaphore_signal(
                    sem, inc=1, device_id=self.device(self.step(at, axis, k)), device_id_type=MESH
                )
                total += 1
        pl.semaphore_wait(sem, total)


def schedule(chunks, stages, skew):
    events = [(ci + skew * s, ci, s) for ci in range(chunks) for s in range(stages)]
    return [(ci, s) for _, ci, s in sorted(events)]


def gather_kernel(grid, chunks, count, *refs):
    ins, outs = refs[:count], refs[count : 2 * count]
    local_sem, send_sem, recv_sem = refs[2 * count :]
    at = grid.here()
    grid.barrier(at)
    locals_ = []
    for i in range(count):
        index = tuple(pl.ds(at[a], 1) for a in "xczy")
        copy = pltpu.make_async_copy(ins[i], outs[i].at[index], local_sem.at[i])
        copy.start()
        locals_.append(copy)
    waited = set()
    number = 0
    flying = {}
    for ci, s in schedule(len(chunks), 5, 1.5):
        array, low, width, order = chunks[ci]
        columns = pl.ds(low, width)
        if s > 0:
            if array not in waited:
                locals_[array].wait()
                waited.add(array)
            for copy in flying[ci, s - 1]:
                copy.wait_recv()
        if s == 4:
            continue
        done = order[:s]
        index = tuple(pl.ds(0, grid.size[a]) if a in done else pl.ds(at[a], 1) for a in "xczy")
        block = outs[array].at[index + (slice(None), columns)]
        source = ins[array].at[:, :, :, :, :, columns] if s == 0 else block
        flying[ci, s] = []
        for k in range(1, grid.size[order[s]]):
            copy = pltpu.make_async_remote_copy(
                src_ref=source,
                dst_ref=block,
                send_sem=send_sem.at[number],
                recv_sem=recv_sem.at[number],
                device_id=grid.device(grid.step(at, order[s], k)),
                device_id_type=MESH,
            )
            copy.start()
            number += 1
            flying[ci, s].append(copy)
    for copies in flying.values():
        for copy in copies:
            copy.wait_send()


def gather_all(grid, arrays, chunks):
    per_chunk = sum(n - 1 for n in grid.size.values())
    copies = per_chunk * len(chunks)
    shaped = [a.reshape((1, 1, 1, 1) + a.shape) for a in arrays]
    return pl.pallas_call(
        functools.partial(gather_kernel, grid, chunks, len(arrays)),
        out_shape=[jax.ShapeDtypeStruct(grid.shape() + a.shape, a.dtype) for a in arrays],
        in_specs=[pl.BlockSpec(memory_space=pl.ANY)] * len(arrays),
        out_specs=[pl.BlockSpec(memory_space=pl.ANY)] * len(arrays),
        scratch_shapes=[
            pltpu.SemaphoreType.DMA((len(arrays),)),
            pltpu.SemaphoreType.DMA((copies,)),
            pltpu.SemaphoreType.DMA((copies,)),
        ],
        compiler_params=pltpu.CompilerParams(collective_id=0, has_side_effects=True),
        name="gather_weights",
    )(*shaped)


def scatter_kernel(grid, chunks, count, *refs):
    ins, outs = refs[:count], refs[count : 2 * count]
    rest = refs[2 * count :]
    held = rest[: len(chunks)]
    landed = rest[len(chunks) : 5 * len(chunks)]
    local_sem, send_sem, recv_sem = rest[5 * len(chunks) :]
    at = grid.here()
    grid.barrier(at)
    number = 0
    flying, locals_ = {}, []
    for ci, s in schedule(len(chunks), 5, 1.5):
        array, low, width, order = chunks[ci]
        columns = pl.ds(low, width)
        if s > 0:
            if s == 1:
                locals_[ci].wait()
            for copy in flying[ci, s - 1]:
                copy.wait_recv()
            done = order[:s]
            arrived = landed[4 * ci + s - 1]
            sizes = [1 if a in done else grid.size[a] for a in "xczy"]
            fixed = [
                0 if a == "c" else (at[a] if a in done else None) for a in "xczy"
            ]
            total = sizes[0] * sizes[1] * sizes[2] * sizes[3]
            peers = grid.size[order[s - 1]] - 1

            def add(i, carry, s=s, ci=ci, array=array, columns=columns, sizes=sizes, fixed=fixed,
                    arrived=arrived, peers=peers):
                place, spot, left = [], [], i
                for n, at_fixed in reversed(list(zip(sizes, fixed))):
                    part = 0 if n == 1 else lax.rem(left, n)
                    left = left if n == 1 else lax.div(left, n)
                    spot.append(part)
                    place.append(part if at_fixed is None else at_fixed)
                place, spot = tuple(reversed(place)), tuple(reversed(spot))
                value = held[ci][place].astype(jnp.float32)
                for k in range(peers):
                    value = value + arrived[(k,) + spot].astype(jnp.float32)
                if s == 4:
                    outs[array][:, columns] = value
                else:
                    held[ci][place] = value.astype(held[ci].dtype)
                return carry

            if total == 1:
                add(0, 0)
            else:
                lax.fori_loop(0, total, add, 0)
        if s == 4:
            continue
        axis = order[s]
        done = order[:s]
        if s == 0:
            index = tuple(pl.ds(at[a], 1) if a == "c" else slice(None) for a in "xczy")
            copy = pltpu.make_async_copy(
                ins[array].at[index + (slice(None), columns)], held[ci], local_sem.at[ci]
            )
            copy.start()
            locals_.append(copy)
        flying[ci, s] = []
        for k in range(1, grid.size[axis]):
            target = grid.step(at, axis, k)
            index = []
            for a in "xczy":
                if a == axis:
                    index.append(pl.ds(target[a], 1))
                elif a in done and a != "c":
                    index.append(pl.ds(at[a], 1))
                else:
                    index.append(slice(None))
            index = tuple(index)
            if s == 0:
                source = ins[array].at[index + (slice(None), columns)]
            else:
                source = held[ci].at[index]
            copy = pltpu.make_async_remote_copy(
                src_ref=source,
                dst_ref=landed[4 * ci + s].at[k - 1],
                send_sem=send_sem.at[number],
                recv_sem=recv_sem.at[number],
                device_id=grid.device(target),
                device_id_type=MESH,
            )
            copy.start()
            number += 1
            flying[ci, s].append(copy)
    for copies in flying.values():
        for copy in copies:
            copy.wait_send()


def scatter_sums(grid, arrays, chunks):
    per_chunk = sum(n - 1 for n in grid.size.values())
    copies = per_chunk * len(chunks)
    held, landed = [], []
    for array, _, width, order in chunks:
        dtype, rows = arrays[array].dtype, arrays[array].shape[-2]
        shape = [1 if a == "c" else grid.size[a] for a in "xczy"] + [rows, width]
        held.append(pltpu.VMEM(tuple(shape), dtype))
        for s in range(4):
            part = [1 if a in order[: s + 1] else grid.size[a] for a in "xczy"] + [rows, width]
            landed.append(pltpu.VMEM((max(grid.size[order[s]] - 1, 1),) + tuple(part), dtype))
    return pl.pallas_call(
        functools.partial(scatter_kernel, grid, chunks, len(arrays)),
        out_shape=[jax.ShapeDtypeStruct(a.shape[-2:], jnp.float32) for a in arrays],
        in_specs=[pl.BlockSpec(memory_space=pl.ANY)] * len(arrays),
        out_specs=[pl.BlockSpec(memory_space=pltpu.VMEM)] * len(arrays),
        scratch_shapes=held
        + landed
        + [
            pltpu.SemaphoreType.DMA((len(chunks),)),
            pltpu.SemaphoreType.DMA((copies,)),
            pltpu.SemaphoreType.DMA((copies,)),
        ],
        compiler_params=pltpu.CompilerParams(
            collective_id=1, has_side_effects=True, vmem_limit_bytes=48 * 1024 * 1024
        ),
        name="scatter_grads",
    )(*arrays)


def swap_halves(values, first_half, half_dim):
    lanes = values.shape[-1]
    down = pltpu.roll(values, lanes - half_dim, 1)
    up = pltpu.roll(values, half_dim, 1)
    return jnp.where(first_half, down, up)


def lane_masks(rows):
    lane = lax.broadcasted_iota(jnp.int32, (rows, LANES), 1)
    return lane, lax.rem(lane, HEAD_DIM) < HEAD_DIM // 2


def forward_kernel(scale, q_ref, k_ref, v_ref, cos_ref, sin_ref, col_ref, row_ref,
                   rq_ref, rk_ref, rv_ref, att_ref, prob_ref):
    rows = q_ref.shape[0]
    lane, first_half = lane_masks(rows)
    cosine, sine = cos_ref[...], sin_ref[...]
    q, k = q_ref[...], k_ref[...]
    half = HEAD_DIM // 2
    rq = (q * cosine + swap_halves(q, first_half, half) * sine).astype(jnp.bfloat16)
    rk = (k * cosine + swap_halves(k, first_half, half) * sine).astype(jnp.bfloat16)
    rv = v_ref[...].astype(jnp.bfloat16)
    rq_ref[...], rk_ref[...], rv_ref[...] = rq, rk, rv
    i = lax.broadcasted_iota(jnp.int32, (rows, rows), 0)
    j = lax.broadcasted_iota(jnp.int32, (rows, rows), 1)
    allowed = (col_ref[...] == row_ref[...]) & (jnp.abs(i - j) <= HALF_WINDOW)
    result = jnp.zeros((rows, LANES), jnp.float32)
    for h in range(LANES // HEAD_DIM):
        mine = lax.div(lane, HEAD_DIM) == h
        scores = times_transposed(jnp.where(mine, rq, jnp.zeros_like(rq)), rk) * scale
        scores = jnp.where(allowed, scores, big_negative)
        top = jnp.max(scores, axis=-1, keepdims=True)
        weights = jnp.exp(scores - top)
        prob = weights * (1.0 / jnp.sum(weights, axis=-1, keepdims=True))
        prob_ref[h] = prob
        part = jnp.dot(prob.astype(jnp.bfloat16), rv, preferred_element_type=jnp.float32)
        result = jnp.where(mine, part, result)
    att_ref[...] = result.astype(jnp.bfloat16)


def backward_kernel(scale, rq_ref, rk_ref, rv_ref, att_ref, datt_ref, prob_ref, cos_ref, sin_ref,
                    out_ref):
    rows = rq_ref.shape[0]
    width = out_ref.shape[1] // 3
    lane, first_half = lane_masks(rows)
    rq, rk, rv, datt = rq_ref[...], rk_ref[...], rv_ref[...], datt_ref[...]
    product = datt.astype(jnp.float32) * att_ref[...].astype(jnp.float32)
    dq = jnp.zeros((rows, LANES), jnp.float32)
    dk, dv = dq, dq
    for h in range(LANES // HEAD_DIM):
        mine = lax.div(lane, HEAD_DIM) == h
        delta = jnp.sum(jnp.where(mine, product, 0.0), axis=-1, keepdims=True)
        dprob = times_transposed(jnp.where(mine, datt, jnp.zeros_like(datt)), rv)
        prob = prob_ref[h]
        dscores = (prob * (dprob - delta) * scale).astype(jnp.bfloat16)
        dv = jnp.where(mine, contract_rows(prob.astype(jnp.bfloat16), datt), dv)
        dq = jnp.where(mine, jnp.dot(dscores, rk, preferred_element_type=jnp.float32), dq)
        dk = jnp.where(mine, contract_rows(dscores, rq), dk)
    cosine, sine = cos_ref[...], sin_ref[...]
    half = HEAD_DIM // 2
    dq = dq * cosine - swap_halves(dq, first_half, half) * sine
    dk = dk * cosine - swap_halves(dk, first_half, half) * sine
    at = pl.program_id(0) * LANES
    for part, value in enumerate((dq, dk, dv)):
        columns = pl.ds(pl.multiple_of(part * width + at, LANES), LANES)
        out_ref[:, columns] = value.astype(jnp.bfloat16)


def attention_forward(projected, cosine, sine, starts, scale):
    rows, width = projected.shape[0], projected.shape[1] // 3
    pairs = width // LANES
    heads = LANES // HEAD_DIM
    block = lambda offset: pl.BlockSpec((rows, LANES), lambda j: (0, j + offset))
    whole = lambda shape: pl.BlockSpec(shape, lambda j: (0, 0))
    wide = jax.ShapeDtypeStruct((rows, width), jnp.bfloat16)
    return pl.pallas_call(
        functools.partial(forward_kernel, scale),
        grid=(pairs,),
        in_specs=[block(0), block(pairs), block(2 * pairs), whole((rows, LANES)),
                  whole((rows, LANES)), whole((rows, 1)), whole((1, rows))],
        out_specs=[block(0)] * 4 + [pl.BlockSpec((heads, rows, rows), lambda j: (j, 0, 0))],
        out_shape=[wide] * 4 + [jax.ShapeDtypeStruct((pairs * heads, rows, rows), jnp.float32)],
        name="attention_forward",
    )(projected, projected, projected, cosine, sine, starts[:, None], starts[None, :])


def attention_backward(rq, rk, rv, attended, d_attended, prob, cosine, sine, scale):
    rows, width = rq.shape
    pairs = width // LANES
    heads = LANES // HEAD_DIM
    block = pl.BlockSpec((rows, LANES), lambda j: (0, j))
    whole = lambda shape: pl.BlockSpec(shape, lambda j: (0, 0))
    return pl.pallas_call(
        functools.partial(backward_kernel, scale),
        grid=(pairs,),
        in_specs=[block] * 5 + [pl.BlockSpec((heads, rows, rows), lambda j: (j, 0, 0)),
                  whole((rows, LANES)), whole((rows, LANES))],
        out_specs=whole((rows, 3 * width)),
        out_shape=jax.ShapeDtypeStruct((rows, 3 * width), jnp.bfloat16),
        name="attention_backward",
    )(rq, rk, rv, attended, d_attended, prob, cosine, sine)


def halves(array, columns, first, second):
    if columns % (2 * LANES):
        return [(array, 0, columns, first)]
    half = columns // 2
    return [(array, 0, half, first), (array, half, half, second)]


def body(
    grid,
    tokens,
    cotangent,
    starts,
    attention_norm_scale,
    w_qkv,
    w_out,
    feedforward_norm_scale,
    w_in,
    w_down,
):
    row_count, width = tokens.shape
    units = w_down.shape[0]
    scale = HEAD_DIM ** (-0.5)
    owned = w_qkv.shape[0]
    devices = width // owned
    axes = ("dp", "fsdp")
    kernels = owned % 8 == 0 and owned <= LANES
    out_t, down_t = w_out.T, w_down.T
    if kernels:
        scales = jnp.pad(
            jnp.stack([attention_norm_scale, feedforward_norm_scale]),
            ((0, 14), (0, LANES - owned)),
        )
        parts = [scales, w_qkv, out_t, w_in, down_t]
        zyx, zxy = ("z", "y", "x", "c"), ("z", "x", "y", "c")
        chunks = [(0, 0, LANES, zyx)]
        chunks += halves(1, w_qkv.shape[1], zyx, zxy)
        chunks += halves(2, width, zyx, zxy)
        chunks += halves(3, w_in.shape[1], zyx, zxy)
        chunks += halves(4, units, zxy, zyx)
        all_scales, full_qkv, full_out_t, full_in, full_down_t = gather_all(grid, parts, chunks)
        all_scales = all_scales.reshape(devices, 16, LANES)
        attention_scale = all_scales[:, 0, :owned].reshape(width)
        feedforward_scale = all_scales[:, 1, :owned].reshape(width)
        full_qkv, full_out_t, full_in, full_down_t = (
            a.reshape(width, a.shape[-1]) for a in (full_qkv, full_out_t, full_in, full_down_t)
        )
    else:
        full_qkv, full_out_t, full_in, full_down_t, attention_scale, feedforward_scale = (
            lax.all_gather(a, axes, axis=0, tiled=True)
            for a in (w_qkv, out_t, w_in, down_t, attention_norm_scale, feedforward_norm_scale)
        )
    attention_scale = attention_scale.astype(jnp.float32)
    feedforward_scale = feedforward_scale.astype(jnp.float32)
    slot = jnp.arange(row_count, dtype=jnp.int32)
    valid = starts < row_count
    position = slot - starts
    input_float = tokens.astype(jnp.float32)
    first_standardized, first_inverse_deviation = apply_layer_norm(input_float)
    first_normalized = (first_standardized * attention_scale).astype(jnp.bfloat16)
    projected = jnp.dot(first_normalized, full_qkv, preferred_element_type=jnp.float32)
    cosine, sine = rotary_tables(position, HEAD_DIM)
    repeats = LANES // HEAD_DIM
    cosine = jnp.tile(jnp.concatenate([cosine, cosine], 1), (1, repeats))
    sine = jnp.tile(jnp.concatenate([-sine, sine], 1), (1, repeats))
    rq, rk, rv, attended, prob = attention_forward(projected, cosine, sine, starts, scale)
    hidden_state = input_float + times_transposed(attended, full_out_t)
    second_standardized, second_inverse_deviation = apply_layer_norm(hidden_state)
    second_normalized = (second_standardized * feedforward_scale).astype(jnp.bfloat16)
    gate_up = jnp.dot(second_normalized, full_in, preferred_element_type=jnp.float32)
    pre_act = gate_up[:, :units]
    gate_half = gate_up[:, units:]
    activated, slope = gelu_parts(pre_act)
    hidden = (activated * gate_half).astype(jnp.bfloat16)
    output = (hidden_state + times_transposed(hidden, full_down_t)).astype(jnp.bfloat16)
    grad_out = jnp.where(valid[:, None], cotangent, jnp.zeros_like(cotangent))
    down_grad_t = contract_rows(grad_out, hidden)
    d_hidden = jnp.dot(grad_out, full_down_t, preferred_element_type=jnp.float32)
    d_gu = jnp.concatenate([d_hidden * gate_half * slope, d_hidden * activated], 1).astype(
        jnp.bfloat16
    )
    second_normalized_gradient = times_transposed(d_gu, full_in)
    mixed_gradient, feedforward_scale_gradient = norm_backward(
        second_normalized_gradient,
        second_standardized,
        second_inverse_deviation,
        feedforward_scale,
    )
    d_state = grad_out.astype(jnp.float32) + mixed_gradient
    d_state_b = d_state.astype(jnp.bfloat16)
    out_grad_t = contract_rows(d_state_b, attended)
    d_attended = jnp.dot(d_state_b, full_out_t, preferred_element_type=jnp.float32).astype(
        jnp.bfloat16
    )
    d_qkv = attention_backward(rq, rk, rv, attended, d_attended, prob, cosine, sine, scale)
    first_normalized_gradient = times_transposed(d_qkv, full_qkv)
    norm_input_gradient, attention_scale_gradient = norm_backward(
        first_normalized_gradient,
        first_standardized,
        first_inverse_deviation,
        attention_scale,
    )
    input_grad = d_state + norm_input_gradient
    qkv_whole = contract_rows(first_normalized, d_qkv)
    in_whole = contract_rows(second_normalized, d_gu)
    every_grad = (in_whole, down_grad_t, out_grad_t, qkv_whole)
    gains = (attention_scale_gradient, feedforward_scale_gradient)
    if kernels:
        gains = jnp.stack(gains).reshape(2, devices, owned).transpose(1, 0, 2)
        gains = jnp.pad(gains, ((0, 0), (0, 6), (0, LANES - owned)))
        parts = [a.astype(jnp.bfloat16).reshape(grid.shape() + (owned, a.shape[-1])) for a in every_grad]
        parts.append(gains.reshape(grid.shape() + (8, LANES)))
        xyz, yxz = ("c", "x", "y", "z"), ("c", "y", "x", "z")
        chunks = halves(0, in_whole.shape[1], xyz, yxz)
        chunks += halves(1, units, xyz, yxz)
        chunks += halves(2, width, yxz, xyz)
        chunks += halves(3, qkv_whole.shape[1], xyz, yxz)
        chunks += [(4, 0, LANES, xyz)]
        in_owned, down_owned_t, out_owned_t, qkv_owned, gains = scatter_sums(grid, parts, chunks)
        gain_a_owned, gain_m_owned = gains[0, :owned], gains[1, :owned]
    else:
        in_owned, down_owned_t, out_owned_t, qkv_owned, gain_a_owned, gain_m_owned = (
            lax.psum_scatter(a, axes, scatter_dimension=0, tiled=True) for a in every_grad + gains
        )
    return (
        output,
        input_grad,
        qkv_owned,
        out_owned_t.T,
        in_owned,
        down_owned_t.T,
        gain_a_owned,
        gain_m_owned,
    )


def solution(mesh):
    return jax.shard_map(
        functools.partial(body, Grid(mesh.shape["dp"], mesh.shape["fsdp"])),
        mesh=mesh,
        in_specs=(
            P(("dp", "fsdp"), None),
            P(("dp", "fsdp"), None),
            P(("dp", "fsdp")),
            P(("dp", "fsdp")),
            P(("dp", "fsdp"), None),
            P(None, ("dp", "fsdp")),
            P(("dp", "fsdp")),
            P(("dp", "fsdp"), None),
            P(None, ("dp", "fsdp")),
        ),
        out_specs=(
            P(("dp", "fsdp"), None),
            P(("dp", "fsdp"), None),
            P(("dp", "fsdp"), None),
            P(None, ("dp", "fsdp")),
            P(("dp", "fsdp"), None),
            P(None, ("dp", "fsdp")),
            P(("dp", "fsdp")),
            P(("dp", "fsdp")),
        ),
        check_vma=False,
    )
```

time: 725 us -> 200 us (0.28)
  waiting for transfers between devices: 457 us -> 0 us
  Pallas kernels: 0 us -> 157 us
  matrix products: 126 us -> 25.8 us
  blocking collectives: 80.8 us -> 0 us
  local copies, waits for them, and re-layouts: 28.3 us -> 8.74 us
  between operations: 14.5 us -> 0.96 us
    reduce_scatter x3 -> x0, waiting for transfers between devices: 250 us -> none  [the longest x1 125 us: body(): lax.psum_scatter(every_grad[0], ('dp', 'fsdp'), scatter_dimension=0, tile...]
    pallas_call x0 -> x4, Pallas kernels: none -> 157 us  [the longest x1 71.5 us: scatter_sums(): pl.pallas_call(functools.partial(scatter_kernel, grid, chunks, len(arrays...]
    all_gather x4 -> x0, waiting for transfers between devices: 154 us -> none  [the longest x1 58.6 us: body(): lax.all_gather(shards[2], ('dp', 'fsdp'), axis=0, tiled=True)]
    dot_general x86 -> x2, matrix products: 93.8 us -> 2.29 us  [the longest x1 1.25 us: body(): jnp.dot(d_state_b, full_out_t, preferred_element_type=jnp.float32)]
    unnamed x2 -> x0, blocking collectives: 80.8 us -> none
    unnamed x9 -> x0, waiting for transfers between devices: 53.2 us -> none
    dynamic_slice x48 -> x0, local copies, waits for them, and re-layouts: 10.9 us -> none  [the longest x12 7.96 us: body(): lax.map(head_backward, (queries, keys_rot, values_h, log_totals, attended...]
  transfers between devices with their start and end apart: 8 -> 0, of which waited for: 7 -> 0; matrix products, arithmetic and copies ran while one was open for 22% -> 0% of each run, Pallas kernels for 0% -> 0%
where the time goes in v1:
time: 200 us; the launch traced here: 199 us
  Pallas kernels  157 us (78%)
  matrix products  25.8 us (13%)
  local copies, waits for them, and re-layouts  8.74 us (4%)
  other arithmetic  7.13 us (4%)
    pallas_call x1, Pallas kernels, scatter_sums(): pl.pallas_call(functools.partial(scatter_kernel, grid, chunks, len(arrays...  71.5 us
    pallas_call x1, Pallas kernels, gather_all(): pl.pallas_call(functools.partial(gather_kernel, grid, chunks, len(arrays)...  67.9 us
    pallas_call x1, Pallas kernels, attention_forward(): pl.pallas_call(functools.partial(forward_kernel, scale), grid=(pairs,), i...  9.4 us
    dot_general x4, matrix products, times_transposed(): lax.dot_general(left, right, (((1,), (1,)), ((), ())), preferred_element_...  9.24 us
    dot_general x4, matrix products, contract_rows(): lax.dot_general(left, right, (((0,), (0,)), ((), ())), preferred_element_...  8.58 us
    pallas_call x1, Pallas kernels, attention_backward(): pl.pallas_call(functools.partial(backward_kernel, scale), grid=(pairs,),...  7.83 us
    dot_general x1, matrix products, body(): jnp.dot(first_normalized, full_qkv, preferred_element_type=jnp.float32)  4.53 us

profile of v1, /device:TPU:0, one launch (start us, length us, event | category | flops | bytes accessed | tf_op | source)
XLA Modules:
  0.0 199.2 jit_solution(4717982108706921783)
XLA Ops:
  2.1 1.1 convert_reduce_fusion
  3.2 1.3 fusion.19
  4.5 1.3 fusion.30.refs_0_
  6.1 0.8 copy.18.cos_ref
  7.6 0.8 copy.20.col_ref
  8.4 67.9 %gather_weights.1 = (bf16[2,2,4,2,16,128]{5,4,3,2,1,0:T(8,128)(2,1)}, bf16[2,2,4,2,24,2304]{5,4,3,2,1,0:T(8,128)(2,1)}, bf16[2,2,4,2,24,768]{5,4,3,2,1,0:T(8,128...) custom-call(bf16[1,1,1,1,16,128]{5,4,3,2,1,0:T(8,128)(2,1)} %fusion.30.refs_0_, ...), custom_call_target="tpu_custom_call" | custom-call | tf_op jit(solution)/shard_map/gather_weights/pallas_call | solution.py:180
  76.3 0.9 fusion.38
  77.4 4.5 %fusion.35.q_ref.k_ref.v_ref = f32[256,2304]{1,0:T(8,128)} fusion(bf16[768,2304]{1,0:T(8,128)(2,1)} %bitcast.61, bf16[256,768]{1,0:T(8,128)(2,1)S(1)} %copy-done, f32[768]{0:T(1024)S(1)} %reshape.152, f32[256]{0:T(256)S(1)} %add_rsqrt_fusion.1, f32[256]{0:T(256)S(1)} %broadcast_multiply_fusion.5), kind=kOutput, calls=%fused_computation.80 | convolution fusion | flops 906952704 | bytes 6296576 | tf_op jit(solution)/shard_map/dot_general | solution.py:479
  82.0 9.4 %attention_forward.1 = (bf16[256,768]{1,0:T(8,128)(2,1)}, bf16[256,768]{1,0:T(8,128)(2,1)}, bf16[256,768]{1,0:T(8,128)(2,1)}, bf16[256,768]{1,0:T(8,128)(2,1)}, f32[12,256,256]{2,1,0:T(8,128)}) custom-call(f32[256,2304]{1,0:T(8,128)} %fusion.35.q_ref.k_ref.v_ref, f32[256,2304]{1,0:T(8,128)} %fusion.35.q_ref.k_ref.v_ref, ...), custom_call_target="tpu_custom_call" | custom-call | tf_op jit(solution)/shard_map/attention_forward/pallas_call | solution.py:392
  91.4 1.7 fusion.39
  93.5 1.2 fusion.37
  95.0 1.0 fusion.6
  96.1 1.5 fusion
  97.6 1.8 multiply_reduce_fusion
  99.8 1.2 convolution_convert_fusion.4.datt_ref
  101.0 7.8 %attention_backward.1 = bf16[256,2304]{1,0:T(8,128)(2,1)} custom-call(bf16[256,768]{1,0:T(8,128)(2,1)} %get-tuple-element.29.rq_ref, bf16[256,768]{1,0:T(8,128)(2,1)} %get-tuple-element.30.rk_ref, bf16[256,768]{1,0:T(8,128)(2,1)} %get-tuple-element.31.rv_ref, bf16[256,768]{1,0:T(8,128)(2,1)} %get-tuple-element.25.att_ref, ...), custom_call_target="tpu_custom_call" | custom-call | tf_op jit(solution)/shard_map/attention_backward/pallas_call | solution.py:409
  108.8 4.2 %fusion.18 = (f32[768]{0:T(1024)}, f32[256]{0:T(256)S(1)}, f32[256]{0:T(256)S(1)}, f32[256,768]{1,0:T(8,128)S(1)}) fusion(bf16[256,768]{1,0:T(8,128)(2,1)S(1)} %copy-done, f32[256]{0:T(256)S(1)} %copy-done.13, f32[256]{0:T(256)S(1)} %broadcast_multiply_fusion.5, f32[768]{0:T(1024)S(1)} %reshape.152, bf16[256,2304]{1,0:T(8,128)(2,1)} %attention_backward.1, ...), kind=kOutput, calls=%fused_computation.33 | convolution fusion | flops 907737856 | bytes 5908480 | tf_op jit(solution)/shard_map/dot_general | solution.py:78
  113.1 1.2 fusion.17
  114.8 0.8 stack.21
  115.6 0.8 stack.22
  116.4 2.0 convolution_convert_fusion.2
  118.5 3.0 %convolution_convert_fusion.1 = bf16[768,2304]{1,0:T(8,128)(2,1)} fusion(bf16[256,1152]{1,0:T(8,128)(2,1)S(1)} %copy-done.11, bf16[256,1152]{1,0:T(8,128)(2,1)S(1)} %copy-done.9, f32[256,768]{1,0:T(8,128)S(1)} %get-tuple-element.55, f32[768]{0:T(1024)S(1)} %reshape.153, f32[256]{0:T(256)S(1)} %copy-done.16, f32[256]{0:T(256)S(1)} %broadcast_multiply_fusion.4), kind=kOutput, calls=%fused_computation.1 | convolution fusion | flops 910884864 | bytes 5510144 | tf_op jit(solution)/shard_map/dot_general | solution.py:72
  121.5 3.1 %convolution_convert_fusion = bf16[768,2304]{1,0:T(8,128)(2,1)} fusion(bf16[256,2304]{1,0:T(8,128)(2,1)S(1)} %copy-done.1, bf16[256,768]{1,0:T(8,128)(2,1)S(1)} %copy-done, f32[768]{0:T(1024)S(1)} %reshape.152, f32[256]{0:T(256)S(1)} %copy-done.14, f32[256]{0:T(256)S(1)} %broadcast_multiply_fusion.5), kind=kOutput, calls=%fused_computation | convolution fusion | flops 908722176 | bytes 5116928 | tf_op jit(solution)/shard_map/dot_general | solution.py:72
  124.6 71.5 %scatter_grads.1 = (f32[24,2304]{1,0:T(8,128)S(1)}, f32[24,1152]{1,0:T(8,128)S(1)}, f32[24,768]{1,0:T(8,128)S(1)}, f32[24,2304]{1,0:T(8,128)S(1)}, f32[8,128]{1,0:T(8,128)S(1)}) custom-call(bf16[2,2,4,2,24,2304]{5,4,3,2,1,0:T(8,128)(2,1)} %bitcast.58, bf16[2,2,4,2,24,1152]{5,4,3,2,1,0:T(8,128)(2,1)S(1)} %bitcast.52, ...), custom_call_target="tpu_custom_call" | custom-call | tf_op jit(solution)/shard_map/scatter_grads/pallas_call | solution.py:298
  (70 shorter events, 7.5 us)
Async XLA Ops:
  0.6 7.0 %copy-start.17 = (s32[256]{0:T(256)S(1)}, s32[256]{0:T(256)}, u32[]{:S(2)}) copy-start(s32[256]{0:T(256)} %param.11) | copy-start | bytes 3076
  1.4 93.3 %copy-start.18 = (pred[256]{0:T(512)(128)(4,1)}, pred[256]{0:T(512)(128)(4,1)S(1)}, u32[]{:S(2)}) copy-start(pred[256]{0:T(512)(128)(4,1)S(1)} %broadcast_compare_fusion) | copy-start | bytes 772
  3.2 74.2 %copy-start = (bf16[256,768]{1,0:T(8,128)(2,1)S(1)}, bf16[256,768]{1,0:T(8,128)(2,1)}, u32[]{:S(2)}) copy-start(bf16[256,768]{1,0:T(8,128)(2,1)} %param.9) | copy-start | bytes 1179652
  4.5 77.4 %copy-start.12 = (f32[256]{0:T(256)}, f32[256]{0:T(256)S(1)}, u32[]{:S(2)}) copy-start(f32[256]{0:T(256)S(1)} %add_rsqrt_fusion.1) | copy-start | bytes 3076
  82.0 9.4 %copy-start.2 = (bf16[2,2,4,2,24,768]{5,4,3,2,1,0:T(8,128)(2,1)S(1)}, bf16[2,2,4,2,24,768]{5,4,3,2,1,0:T(8,128)(2,1)}, u32[]{:S(2)}) copy-start(bf16[2,2,4,2,24,768]{5,4,3,2,1,0:T(8,128)(2,1)} %get-tuple-element.26) | copy-start | bytes 3538948
  91.4 2.1 %copy-start.4 = (bf16[2,2,4,2,24,2304]{5,4,3,2,1,0:T(8,128)(2,1)S(1)}, bf16[2,2,4,2,24,2304]{5,4,3,2,1,0:T(8,128)(2,1)}, u32[]{:S(2)}) copy-start(bf16[2,2,4,2,24,2304]{5,4,3,2,1,0:T(8,128)(2,1)} %get-tuple-element.27) | copy-start | bytes 10616836
  93.5 5.9 %copy-start.15 = (f32[256]{0:T(256)}, f32[256]{0:T(256)S(1)}, u32[]{:S(2)}) copy-start(f32[256]{0:T(256)S(1)} %add_rsqrt_fusion) | copy-start | bytes 3076
  93.5 1.5 copy-start.6
  93.5 1.5 copy-start.7
  96.1 1.5 copy-start.5
  96.1 1.5 copy-start.8
  96.1 1.5 copy-start.10
  97.6 1.8 copy-start.19
  101.0 7.8 %copy-start.13 = (f32[256]{0:T(256)S(1)}, f32[256]{0:T(256)}, u32[]{:S(2)}) copy-start(f32[256]{0:T(256)} %copy-done.12) | copy-start | bytes 3076
  113.1 1.2 copy-start.3
  116.4 2.0 %copy-start.9 = (bf16[256,1152]{1,0:T(8,128)(2,1)S(1)}, bf16[256,1152]{1,0:T(8,128)(2,1)}, u32[]{:S(2)}) copy-start(bf16[256,1152]{1,0:T(8,128)(2,1)} %copy-done.8) | copy-start | bytes 1769476
  116.4 2.0 %copy-start.11 = (bf16[256,1152]{1,0:T(8,128)(2,1)S(1)}, bf16[256,1152]{1,0:T(8,128)(2,1)}, u32[]{:S(2)}) copy-start(bf16[256,1152]{1,0:T(8,128)(2,1)} %copy-done.10) | copy-start | bytes 1769476
  116.4 2.0 %copy-start.16 = (f32[256]{0:T(256)S(1)}, f32[256]{0:T(256)}, u32[]{:S(2)}) copy-start(f32[256]{0:T(256)} %copy-done.15) | copy-start | bytes 3076
  118.4 3.0 %copy-start.1 = (bf16[256,2304]{1,0:T(8,128)(2,1)S(1)}, bf16[256,2304]{1,0:T(8,128)(2,1)}, u32[]{:S(2)}) copy-start(bf16[256,2304]{1,0:T(8,128)(2,1)} %attention_backward.1) | copy-start | bytes 3538948
  118.5 3.0 %copy-start.14 = (f32[256]{0:T(256)S(1)}, f32[256]{0:T(256)}, u32[]{:S(2)}) copy-start(f32[256]{0:T(256)} %copy-done.12) | copy-start | bytes 3076

commit v2 on v1

--- a/solution.py
+++ b/solution.py
@@ -140,7 +140,7 @@
     waited = set()
     number = 0
     flying = {}
-    for ci, s in schedule(len(chunks), 5, 1.5):
+    for ci, s in schedule(len(chunks), 5, 6):
         array, low, width, order = chunks[ci]
         columns = pl.ds(low, width)
         if s > 0:
@@ -202,7 +202,7 @@
     grid.barrier(at)
     number = 0
     flying, locals_ = {}, []
-    for ci, s in schedule(len(chunks), 5, 1.5):
+    for ci, s in schedule(len(chunks), 5, 3):
         array, low, width, order = chunks[ci]
         columns = pl.ds(low, width)
         if s > 0:
@@ -417,11 +417,17 @@
     )(rq, rk, rv, attended, d_attended, prob, cosine, sine)
 
 
-def halves(array, columns, first, second):
-    if columns % (2 * LANES):
-        return [(array, 0, columns, first)]
-    half = columns // 2
-    return [(array, 0, half, first), (array, half, half, second)]
+PIECE = 384
+GATHER_CYCLE = ('zyxc', 'zxyc', 'zyxc', 'zxyc', 'yzxc', 'xzyc')
+SCATTER_CYCLE = ('cxyz', 'cyxz')
+
+
+def pieces(array, columns, orders):
+    piece = PIECE if columns % PIECE == 0 else columns
+    return [
+        (array, low, piece, tuple(orders[n % len(orders)]))
+        for n, low in enumerate(range(0, columns, piece))
+    ]
 
 
 def body(
@@ -450,12 +456,11 @@
             ((0, 14), (0, LANES - owned)),
         )
         parts = [scales, w_qkv, out_t, w_in, down_t]
-        zyx, zxy = ("z", "y", "x", "c"), ("z", "x", "y", "c")
-        chunks = [(0, 0, LANES, zyx)]
-        chunks += halves(1, w_qkv.shape[1], zyx, zxy)
-        chunks += halves(2, width, zyx, zxy)
-        chunks += halves(3, w_in.shape[1], zyx, zxy)
-        chunks += halves(4, units, zxy, zyx)
+        chunks = [(0, 0, LANES, tuple(GATHER_CYCLE[0]))]
+        chunks += pieces(1, w_qkv.shape[1], GATHER_CYCLE)
+        chunks += pieces(2, width, GATHER_CYCLE)
+        chunks += pieces(3, w_in.shape[1], GATHER_CYCLE)
+        chunks += pieces(4, units, GATHER_CYCLE)
         all_scales, full_qkv, full_out_t, full_in, full_down_t = gather_all(grid, parts, chunks)
         all_scales = all_scales.reshape(devices, 16, LANES)
         attention_scale = all_scales[:, 0, :owned].reshape(width)
@@ -528,12 +533,11 @@
         gains = jnp.pad(gains, ((0, 0), (0, 6), (0, LANES - owned)))
         parts = [a.astype(jnp.bfloat16).reshape(grid.shape() + (owned, a.shape[-1])) for a in every_grad]
         parts.append(gains.reshape(grid.shape() + (8, LANES)))
-        xyz, yxz = ("c", "x", "y", "z"), ("c", "y", "x", "z")
-        chunks = halves(0, in_whole.shape[1], xyz, yxz)
-        chunks += halves(1, units, xyz, yxz)
-        chunks += halves(2, width, yxz, xyz)
-        chunks += halves(3, qkv_whole.shape[1], xyz, yxz)
-        chunks += [(4, 0, LANES, xyz)]
+        chunks = pieces(0, in_whole.shape[1], SCATTER_CYCLE)
+        chunks += pieces(1, units, SCATTER_CYCLE)
+        chunks += pieces(2, width, SCATTER_CYCLE)
+        chunks += pieces(3, qkv_whole.shape[1], SCATTER_CYCLE)
+        chunks += [(4, 0, LANES, tuple(SCATTER_CYCLE[0]))]
         in_owned, down_owned_t, out_owned_t, qkv_owned, gains = scatter_sums(grid, parts, chunks)
         gain_a_owned, gain_m_owned = gains[0, :owned], gains[1, :owned]
     else:

time: 200 us -> 177 us (0.89)
  Pallas kernels: 157 us -> 134 us
    pallas_call x1, Pallas kernels: 71.5 us -> 59.5 us  [scatter_sums(): pl.pallas_call(functools.partial(scatter_kernel, grid, chunks, len(arrays...]
    pallas_call x1, Pallas kernels: 67.9 us -> 57.4 us  [gather_all(): pl.pallas_call(functools.partial(gather_kernel, grid, chunks, len(arrays)...]
where the time goes in v2:
time: 177 us
  Pallas kernels  134 us (76%)
  matrix products  25.8 us (15%)
  local copies, waits for them, and re-layouts  8.74 us (5%)
  other arithmetic  7.13 us (4%)
    pallas_call x1, Pallas kernels, scatter_sums(): pl.pallas_call(functools.partial(scatter_kernel, grid, chunks, len(arrays...  59.5 us
    pallas_call x1, Pallas kernels, gather_all(): pl.pallas_call(functools.partial(gather_kernel, grid, chunks, len(arrays)...  57.4 us
    pallas_call x1, Pallas kernels, attention_forward(): pl.pallas_call(functools.partial(forward_kernel, scale), grid=(pairs,), i...  9.4 us
    dot_general x4, matrix products, times_transposed(): lax.dot_general(left, right, (((1,), (1,)), ((), ())), preferred_element_...  9.24 us
    dot_general x4, matrix products, contract_rows(): lax.dot_general(left, right, (((0,), (0,)), ((), ())), preferred_element_...  8.58 us
    pallas_call x1, Pallas kernels, attention_backward(): pl.pallas_call(functools.partial(backward_kernel, scale), grid=(pairs,),...  7.83 us
    dot_general x1, matrix products, body(): jnp.dot(first_normalized, full_qkv, preferred_element_type=jnp.float32)  4.53 us

profile of v2, /device:TPU:0, one launch (start us, length us, event | category | flops | bytes accessed | tf_op | source)
XLA Modules:
  0.0 176.7 jit_solution(18342186472334730833)
XLA Ops:
  2.1 1.1 convert_reduce_fusion
  3.2 1.3 fusion.19
  4.5 1.3 fusion.30.refs_0_
  6.8 0.8 copy.19.sin_ref
  7.6 0.8 copy.20.col_ref
  8.4 57.4 %gather_weights.1 = (bf16[2,2,4,2,16,128]{5,4,3,2,1,0:T(8,128)(2,1)}, bf16[2,2,4,2,24,2304]{5,4,3,2,1,0:T(8,128)(2,1)}, bf16[2,2,4,2,24,768]{5,4,3,2,1,0:T(8,128...) custom-call(bf16[1,1,1,1,16,128]{5,4,3,2,1,0:T(8,128)(2,1)} %fusion.30.refs_0_, ...), custom_call_target="tpu_custom_call" | custom-call | tf_op jit(solution)/shard_map/gather_weights/pallas_call | solution.py:180
  65.8 0.9 fusion.38
  66.9 4.5 %fusion.35.q_ref.k_ref.v_ref = f32[256,2304]{1,0:T(8,128)} fusion(bf16[768,2304]{1,0:T(8,128)(2,1)} %bitcast.61, bf16[256,768]{1,0:T(8,128)(2,1)S(1)} %copy-done, f32[768]{0:T(1024)S(1)} %reshape.152, f32[256]{0:T(256)S(1)} %add_rsqrt_fusion.1, f32[256]{0:T(256)S(1)} %broadcast_multiply_fusion.5), kind=kOutput, calls=%fused_computation.80 | convolution fusion | flops 906952704 | bytes 6296576 | tf_op jit(solution)/shard_map/dot_general | solution.py:484
  71.4 9.4 %attention_forward.1 = (bf16[256,768]{1,0:T(8,128)(2,1)}, bf16[256,768]{1,0:T(8,128)(2,1)}, bf16[256,768]{1,0:T(8,128)(2,1)}, bf16[256,768]{1,0:T(8,128)(2,1)}, f32[12,256,256]{2,1,0:T(8,128)}) custom-call(f32[256,2304]{1,0:T(8,128)} %fusion.35.q_ref.k_ref.v_ref, f32[256,2304]{1,0:T(8,128)} %fusion.35.q_ref.k_ref.v_ref, ...), custom_call_target="tpu_custom_call" | custom-call | tf_op jit(solution)/shard_map/attention_forward/pallas_call | solution.py:392
  80.9 1.7 fusion.39
  83.0 1.2 fusion.37
  84.5 1.0 fusion.6
  85.6 1.5 fusion
  87.1 1.8 %multiply_reduce_fusion = (f32[768]{0:T(1024)}, f32[256]{0:T(256)S(1)}, f32[256]{0:T(256)S(1)}, f32[256,768]{1,0:T(8,128)S(1)}) fusion(f32[256,768]{1,0:T(8,128)S(1)} %get-tuple-element.55, f32[256]{0:T(256)S(1)} %add_rsqrt_fusion, f32[256]{0:T(256)S(1)} %broadcast_multiply_fusion.4, f32[768]{0:T(1024)S(1)} %reshape.153, ...), kind=kOutput, calls=%fused_computation.35 | convolution fusion | flops 909900544 | bytes 6301696 | tf_op jit(solution)/shard_map/dot_general | solution.py:78
  89.2 1.2 convolution_convert_fusion.4.datt_ref
  90.5 7.8 %attention_backward.1 = bf16[256,2304]{1,0:T(8,128)(2,1)} custom-call(bf16[256,768]{1,0:T(8,128)(2,1)} %get-tuple-element.29.rq_ref, bf16[256,768]{1,0:T(8,128)(2,1)} %get-tuple-element.30.rk_ref, bf16[256,768]{1,0:T(8,128)(2,1)} %get-tuple-element.31.rv_ref, bf16[256,768]{1,0:T(8,128)(2,1)} %get-tuple-element.25.att_ref, ...), custom_call_target="tpu_custom_call" | custom-call | tf_op jit(solution)/shard_map/attention_backward/pallas_call | solution.py:409
  98.3 4.2 %fusion.18 = (f32[768]{0:T(1024)}, f32[256]{0:T(256)S(1)}, f32[256]{0:T(256)S(1)}, f32[256,768]{1,0:T(8,128)S(1)}) fusion(bf16[256,768]{1,0:T(8,128)(2,1)S(1)} %copy-done, f32[256]{0:T(256)S(1)} %copy-done.13, f32[256]{0:T(256)S(1)} %broadcast_multiply_fusion.5, f32[768]{0:T(1024)S(1)} %reshape.152, bf16[256,2304]{1,0:T(8,128)(2,1)} %attention_backward.1, ...), kind=kOutput, calls=%fused_computation.33 | convolution fusion | flops 907737856 | bytes 5908480 | tf_op jit(solution)/shard_map/dot_general | solution.py:78
  102.5 1.2 fusion.17
  104.3 0.8 stack.21
  105.0 0.8 stack.22
  105.9 2.0 %convolution_convert_fusion.2 = bf16[768,1152]{1,0:T(8,128)(2,1)S(1)} fusion(bf16[256,1152]{1,0:T(8,128)(2,1)} %copy-done.5, bf16[256,768]{1,0:T(8,128)(2,1)S(1)} %copy-done.7, pred[256]{0:T(512)(128)(4,1)} %copy-done.18), kind=kOutput, calls=%fused_computation.2 | convolution fusion | flops 454066176 | bytes 2752768 | tf_op jit(solution)/shard_map/dot_general | solution.py:72
  107.9 3.0 %convolution_convert_fusion.1 = bf16[768,2304]{1,0:T(8,128)(2,1)} fusion(bf16[256,1152]{1,0:T(8,128)(2,1)S(1)} %copy-done.11, bf16[256,1152]{1,0:T(8,128)(2,1)S(1)} %copy-done.9, f32[256,768]{1,0:T(8,128)S(1)} %get-tuple-element.55, f32[768]{0:T(1024)S(1)} %reshape.153, f32[256]{0:T(256)S(1)} %copy-done.16, f32[256]{0:T(256)S(1)} %broadcast_multiply_fusion.4), kind=kOutput, calls=%fused_computation.1 | convolution fusion | flops 910884864 | bytes 5510144 | tf_op jit(solution)/shard_map/dot_general | solution.py:72
  111.0 3.1 %convolution_convert_fusion = bf16[768,2304]{1,0:T(8,128)(2,1)} fusion(bf16[256,2304]{1,0:T(8,128)(2,1)S(1)} %copy-done.1, bf16[256,768]{1,0:T(8,128)(2,1)S(1)} %copy-done, f32[768]{0:T(1024)S(1)} %reshape.152, f32[256]{0:T(256)S(1)} %copy-done.14, f32[256]{0:T(256)S(1)} %broadcast_multiply_fusion.5), kind=kOutput, calls=%fused_computation | convolution fusion | flops 908722176 | bytes 5116928 | tf_op jit(solution)/shard_map/dot_general | solution.py:72
  114.0 59.5 %scatter_grads.1 = (f32[24,2304]{1,0:T(8,128)S(1)}, f32[24,1152]{1,0:T(8,128)S(1)}, f32[24,768]{1,0:T(8,128)S(1)}, f32[24,2304]{1,0:T(8,128)S(1)}, f32[8,128]{1,0:T(8,128)S(1)}) custom-call(bf16[2,2,4,2,24,2304]{5,4,3,2,1,0:T(8,128)(2,1)} %bitcast.58, bf16[2,2,4,2,24,1152]{5,4,3,2,1,0:T(8,128)(2,1)S(1)} %bitcast.52, ...), custom_call_target="tpu_custom_call" | custom-call | tf_op jit(solution)/shard_map/scatter_grads/pallas_call | solution.py:298
  (70 shorter events, 7.5 us)
Async XLA Ops:
  0.6 7.0 %copy-start.17 = (s32[256]{0:T(256)S(1)}, s32[256]{0:T(256)}, u32[]{:S(2)}) copy-start(s32[256]{0:T(256)} %param.11) | copy-start | bytes 3076
  1.4 82.7 %copy-start.18 = (pred[256]{0:T(512)(128)(4,1)}, pred[256]{0:T(512)(128)(4,1)S(1)}, u32[]{:S(2)}) copy-start(pred[256]{0:T(512)(128)(4,1)S(1)} %broadcast_compare_fusion) | copy-start | bytes 772
  3.2 63.7 %copy-start = (bf16[256,768]{1,0:T(8,128)(2,1)S(1)}, bf16[256,768]{1,0:T(8,128)(2,1)}, u32[]{:S(2)}) copy-start(bf16[256,768]{1,0:T(8,128)(2,1)} %param.9) | copy-start | bytes 1179652
  4.5 66.9 %copy-start.12 = (f32[256]{0:T(256)}, f32[256]{0:T(256)S(1)}, u32[]{:S(2)}) copy-start(f32[256]{0:T(256)S(1)} %add_rsqrt_fusion.1) | copy-start | bytes 3076
  71.4 9.4 %copy-start.2 = (bf16[2,2,4,2,24,768]{5,4,3,2,1,0:T(8,128)(2,1)S(1)}, bf16[2,2,4,2,24,768]{5,4,3,2,1,0:T(8,128)(2,1)}, u32[]{:S(2)}) copy-start(bf16[2,2,4,2,24,768]{5,4,3,2,1,0:T(8,128)(2,1)} %get-tuple-element.26) | copy-start | bytes 3538948
  80.8 2.1 %copy-start.4 = (bf16[2,2,4,2,24,2304]{5,4,3,2,1,0:T(8,128)(2,1)S(1)}, bf16[2,2,4,2,24,2304]{5,4,3,2,1,0:T(8,128)(2,1)}, u32[]{:S(2)}) copy-start(bf16[2,2,4,2,24,2304]{5,4,3,2,1,0:T(8,128)(2,1)} %get-tuple-element.27) | copy-start | bytes 10616836
  83.0 5.9 %copy-start.15 = (f32[256]{0:T(256)}, f32[256]{0:T(256)S(1)}, u32[]{:S(2)}) copy-start(f32[256]{0:T(256)S(1)} %add_rsqrt_fusion) | copy-start | bytes 3076
  83.0 1.5 copy-start.6
  83.0 1.5 copy-start.7
  85.5 1.5 copy-start.5
  85.6 1.5 copy-start.8
  85.6 1.5 copy-start.10
  87.1 1.8 %copy-start.19 = (pred[256]{0:T(512)(128)(4,1)S(1)}, pred[256]{0:T(512)(128)(4,1)}, u32[]{:S(2)}) copy-start(pred[256]{0:T(512)(128)(4,1)} %copy-done.18) | copy-start | bytes 772
  90.5 7.8 %copy-start.13 = (f32[256]{0:T(256)S(1)}, f32[256]{0:T(256)}, u32[]{:S(2)}) copy-start(f32[256]{0:T(256)} %copy-done.12) | copy-start | bytes 3076
  102.5 1.2 copy-start.3
  105.9 2.0 %copy-start.9 = (bf16[256,1152]{1,0:T(8,128)(2,1)S(1)}, bf16[256,1152]{1,0:T(8,128)(2,1)}, u32[]{:S(2)}) copy-start(bf16[256,1152]{1,0:T(8,128)(2,1)} %copy-done.8) | copy-start | bytes 1769476
  105.9 2.0 %copy-start.11 = (bf16[256,1152]{1,0:T(8,128)(2,1)S(1)}, bf16[256,1152]{1,0:T(8,128)(2,1)}, u32[]{:S(2)}) copy-start(bf16[256,1152]{1,0:T(8,128)(2,1)} %copy-done.10) | copy-start | bytes 1769476
  105.9 2.0 %copy-start.16 = (f32[256]{0:T(256)S(1)}, f32[256]{0:T(256)}, u32[]{:S(2)}) copy-start(f32[256]{0:T(256)} %copy-done.15) | copy-start | bytes 3076
  107.9 3.0 %copy-start.1 = (bf16[256,2304]{1,0:T(8,128)(2,1)S(1)}, bf16[256,2304]{1,0:T(8,128)(2,1)}, u32[]{:S(2)}) copy-start(bf16[256,2304]{1,0:T(8,128)(2,1)} %attention_backward.1) | copy-start | bytes 3538948
  107.9 3.0 %copy-start.14 = (f32[256]{0:T(256)S(1)}, f32[256]{0:T(256)}, u32[]{:S(2)}) copy-start(f32[256]{0:T(256)} %copy-done.12) | copy-start | bytes 3076
